TPU v7x, 32 devices: a whole 2x2x4 slice. The times are simulated.
32 devices in a mesh: group: 2 (over y), seq: 4 (over z), tensor: 4 (over x, core).
Axes of the slice: x: 2, y: 2, z: 4, core: 2. Of those that a mesh axis runs over, the one named last changes fastest.
Arguments:
- spans: bfloat16 [1024, 3072], P(('group', 'seq')), parts along dimension 0, may hold values from -6 to 6
- w_in: bfloat16 [3072, 1024], P(None, 'tensor'), may hold values from -0.109375 to 0.109375
- band_weights: bfloat16 [4096, 128], P(('group', 'seq')), parts along dimension 0
- offsets: int32 [32], P(('group', 'seq')), parts along dimension 0, may hold values from 0 to 384, as said below
- w_up: bfloat16 [1024, 4096], P(None, 'tensor'), may hold values from -0.1875 to 0.1875
- d_up: bfloat16 [4096, 4096], P(('group', 'seq'), 'tensor'), parts along dimension 0, may hold values from -3 to 3
Outputs:
- up_proj: bfloat16 [4096, 4096], P(('group', 'seq'), 'tensor'), parts along dimension 0
- d_spans: bfloat16 [1024, 3072], P(('group', 'seq'), 'tensor'), parts along dimension 0
There are 2 independent parts, one for each index of `group`. A program takes and returns all parts, laid end to end along the dimension named above; an argument that names none is the same for every part. Nothing has to cross between parts.
Inputs may be any that keep to these rules, and one draw needn't show every extreme that they name: offsets[b] differs from b * 384 // 15 by at most 128, and both differences -128 and +128 occur in every draw; offsets[0] = 0 and offsets[15] = 384. Hence the bands of the bytes of seq index i lie within the span rows of seq indices i - 3 to i + 3.
All inputs are finite; a program needn't handle non-finite values.
Results may differ from a plain program's by a relative error of at most 0.0058.
Values may be sent and summed in bfloat16 or wider, within the bound.
No kernel may reach another device: no remote copies, remote signals or barrier semaphores. Data moves between devices by JAX's collectives and lax.ppermute only.
A program may use at most 64 MiB of HBM per device.

v0:
```python
import jax
import jax.numpy as jnp
from jax import lax
from jax.sharding import PartitionSpec as P


def band_matrix(band_weights, offsets, anchor, length):
    blocks = offsets.shape[0]
    breadth = band_weights.shape[1]
    band_cube = band_weights.reshape(blocks, -1, breadth)
    relative = anchor + jnp.arange(length, dtype=jnp.int32)[None, :] - offsets[:, None]
    picker = (relative[:, None, :] == jnp.arange(breadth, dtype=jnp.int32)[None, :, None]).astype(
        jnp.bfloat16
    )
    spread = jnp.einsum("bij,bjr->bir", band_cube, picker, preferred_element_type=jnp.float32)
    return spread.astype(jnp.bfloat16).reshape(-1, length)


def touches(offsets, breadth, anchor, length):
    return jnp.any((offsets < anchor + length) & (offsets + breadth > anchor))


def body(spans, w_in, band_weights, offsets, w_up, d_up):
    breadth = band_weights.shape[1]
    reduced = jnp.dot(spans, w_in, preferred_element_type=jnp.float32).astype(jnp.bfloat16)
    feature_count = reduced.shape[1]
    span_rows = reduced.shape[0]
    initial = jnp.zeros((band_weights.shape[0], feature_count), jnp.float32)
    shard_rows = lax.all_gather(reduced, "seq", axis=0, tiled=True)
    anchor = jnp.int32(0)
    length = shard_rows.shape[0]

    def accumulate(current):
        spread = band_matrix(band_weights, offsets, anchor, length)
        return jnp.dot(spread, shard_rows, preferred_element_type=jnp.float32)

    def unchanged(current):
        return current

    upsampled = lax.cond(
        touches(offsets, breadth, anchor, length), accumulate, unchanged, initial
    ).astype(jnp.bfloat16)
    gathered = lax.all_gather(upsampled, "tensor", axis=1, tiled=True)
    up_proj = jnp.dot(gathered, w_up, preferred_element_type=jnp.float32).astype(jnp.bfloat16)
    grad_cols = lax.psum_scatter(
        lax.dot_general(w_up, d_up, (((1,), (1,)), ((), ())), preferred_element_type=jnp.float32),
        "tensor",
        scatter_dimension=0,
        tiled=True,
    ).astype(jnp.bfloat16)

    def compute(operand):
        spread = band_matrix(band_weights, offsets, 0, span_rows * lax.axis_size("seq"))
        return lax.dot_general(
            spread, grad_cols, (((0,), (1,)), ((), ())), preferred_element_type=jnp.float32
        )

    def nothing(operand):
        return jnp.zeros((span_rows * lax.axis_size("seq"), feature_count), jnp.float32)

    every_row = lax.psum(
        lax.cond(
            touches(offsets, breadth, 0, span_rows * lax.axis_size("seq")), compute, nothing, 0
        ),
        "seq",
    )
    d_reduced = lax.dynamic_slice_in_dim(every_row, lax.axis_index("seq") * span_rows, span_rows, 0)
    d_reduced = d_reduced.astype(jnp.bfloat16)
    feature_parts = lax.dot_general(
        d_reduced, w_in, (((1,), (1,)), ((), ())), preferred_element_type=jnp.float32
    )
    d_spans = lax.psum_scatter(feature_parts, "tensor", scatter_dimension=1, tiled=True).astype(
        jnp.bfloat16
    )
    return (up_proj, d_spans)


def solution(mesh):
    placed = (
        P(("group", "seq"), None),
        P(None, "tensor"),
        P(("group", "seq"), None),
        P(("group", "seq")),
        P(None, "tensor"),
        P(("group", "seq"), "tensor"),
    )
    return jax.shard_map(
        body,
        mesh=mesh,
        in_specs=placed,
        out_specs=(P(("group", "seq"), "tensor"), P(("group", "seq"), "tensor")),
        check_vma=False,
    )
```

profile of v0, /device:TPU:0, one launch (start us, length us, event | category | flops | bytes accessed | tf_op | source)
XLA Modules:
  0.0 116.6 jit_solution(14578127177563211295)
XLA Ops:
  7.2 1.5 %copy-done = bf16[1024,1024]{1,0:T(8,128)(2,1)S(1)} copy-done((bf16[1024,1024]{1,0:T(8,128)(2,1)S(1)}, bf16[1024,1024]{1,0:T(8,128)(2,1)}, u32[]{:S(2)}) %copy-start) | copy-done | bytes 2097176
  8.8 3.9 %fusion.6 = f32[1024,512]{1,0:T(8,128)} fusion(bf16[1024,1024]{1,0:T(8,128)(2,1)S(1)} %copy-done, bf16[512,1024]{1,0:T(8,128)(2,1)} %param.15), kind=kOutput, calls=%fused_computation.16 | convolution fusion | flops 1073741824 | bytes 5242880 | tf_op jit(solution)/shard_map/dot_general | solution.py:46
  12.7 0.0 all-gather.2.cloned.1.call-start
  12.7 0.6 copy-done.4
  13.3 0.6 and_reduce_fusion
  14.6 1.8 %convolution_convert_fusion.3 = bf16[128,256]{1,0:T(8,128)(2,1)S(1)} fusion(bf16[128,3072]{1,0:T(8,128)(2,1)S(1)} %copy-done.2, bf16[3072,256]{1,0:T(8,128)(2,1)} %param.11), kind=kOutput, calls=%fused_computation.9 | convolution fusion | flops 201359360 | bytes 2424832 | tf_op jit(solution)/shard_map/dot_general | solution.py:25
  16.4 15.6 %all_gather.6 = bf16[512,256]{1,0:T(8,128)(2,1)S(1)} all-gather(bf16[128,256]{1,0:T(8,128)(2,1)S(1)} %convolution_convert_fusion.3), channel_id=1, replica_groups=mesh['group'=2,'seq'=4,'tensor'=4] {'seq'}, dimensions={0}, use_global_device_ids=true | all-gather | bytes 327680 | tf_op jit(solution)/shard_map/all_gather | solution.py:29
  32.0 0.7 conditional.2
  32.0 0.1 iota_subtract_fusion
  32.1 0.3 convolution_convert_fusion
  32.4 0.3 fusion.4
  32.7 0.7 copy-done.1
  33.5 0.0 reduce-scatter.5.cloned.1.call-start
  33.5 13.4 %reduce-scatter.3.cloned.1.call-done = f32[256,512]{1,0:T(8,128)} async-done(((f32[1024,512]{1,0:T(8,128)}), f32[256,512]{1,0:T(8,128)}) %reduce-scatter.3.cloned.1.call-update) | async-done | bytes 524304 | tf_op jit(solution)/shard_map/reduce_scatter | solution.py:45
  46.9 1.1 convert_element_type.40
  48.0 0.8 conditional.3
  48.0 0.1 iota_subtract_fusion.1
  48.1 0.3 convolution_convert_fusion.1
  48.5 0.3 fusion.5
  48.8 30.5 %all-reduce.1 = bf16[512,256]{1,0:T(8,128)(2,1)S(1)} all-reduce(f32[512,256]{1,0:T(8,128)S(1)} %get-tuple-element.27), channel_id=1, replica_groups=mesh['group'=2,'seq'=4,'tensor'=4] {'seq'}, use_global_device_ids=true, to_apply=%region_6.0 | all-reduce | flops 131072 | bytes 786432 | tf_op jit(solution)/shard_map/psum | solution.py:61
  79.3 3.2 %fusion.2 = f32[128,3072]{1,0:T(8,128)} fusion(bf16[3072,256]{1,0:T(8,128)(2,1)} %param.11, bf16[512,256]{1,0:T(8,128)(2,1)S(1)} %all-reduce.1, s32[]{:T(128)S(6)} %select_n.3), kind=kOutput, calls=%fused_computation.11 | convolution fusion | flops 201326592 | bytes 3211268 | tf_op jit(solution)/shard_map/dot_general | solution.py:69
  82.5 3.4 %convolution_convert_fusion.2 = bf16[512,1024]{1,0:T(8,128)(2,1)} fusion(bf16[512,1024]{1,0:T(8,128)(2,1)} %all-gather.2.cloned.1.call-done, bf16[1024,1024]{1,0:T(8,128)(2,1)S(1)} %copy-done), kind=kOutput, calls=%fused_computation.8 | convolution fusion | flops 1074266112 | bytes 4194304 | tf_op jit(solution)/shard_map/dot_general | solution.py:44
  86.0 22.4 %reduce-scatter.5.cloned.1.call-done = f32[128,768]{1,0:T(8,128)} async-done(((f32[128,3072]{1,0:T(8,128)}), f32[128,768]{1,0:T(8,128)}) %reduce-scatter.5.cloned.1.call-update) | async-done | bytes 393232 | tf_op jit(solution)/shard_map/reduce_scatter | solution.py:72
  108.4 1.7 %convert_element_type.42 = bf16[128,768]{1,0:T(8,128)(2,1)} convert(f32[128,768]{1,0:T(8,128)} %reduce-scatter.5.cloned.1.call-done) | non-fusion elementwise | flops 98304 | bytes 589824 | tf_op jit(solution)/shard_map/convert_element_type | solution.py:72
  (12 shorter events, 0.1 us)
Async XLA Ops:
  7.2 1.6 %copy-start = (bf16[1024,1024]{1,0:T(8,128)(2,1)S(1)}, bf16[1024,1024]{1,0:T(8,128)(2,1)}, u32[]{:S(2)}) copy-start(bf16[1024,1024]{1,0:T(8,128)(2,1)} %param.14) | copy-start | bytes 6291460
  7.2 39.8 %reduce-scatter.3.cloned.1.call-start = ((), (), s32[]{:S(2)}) async-start(), calls=%async_computation.3 | async-start | bytes 2621440 | tf_op jit(solution)/shard_map/reduce_scatter | solution.py:45
  12.6 0.7 copy-start.4
  12.6 1.9 %copy-start.2 = (bf16[128,3072]{1,0:T(8,128)(2,1)S(1)}, bf16[128,3072]{1,0:T(8,128)(2,1)}, u32[]{:S(2)}) copy-start(bf16[128,3072]{1,0:T(8,128)(2,1)} %param.10) | copy-start | bytes 2359300
  12.6 19.4 %copy-start.3 = (bf16[512,128]{1,0:T(8,128)(2,1)S(1)}, bf16[512,128]{1,0:T(8,128)(2,1)}, u32[]{:S(2)}) copy-start(bf16[512,128]{1,0:T(8,128)(2,1)} %param.12) | copy-start | bytes 393220
  12.7 69.9 %all-gather.2.cloned.1.call-start = ((), (), s32[]{:S(2)}) async-start(), calls=%async_computation.2 | async-start | bytes 1310720 | tf_op jit(solution)/shard_map/all_gather | solution.py:43
  32.7 0.7 copy-start.1
  33.5 74.9 %reduce-scatter.5.cloned.1.call-start = ((), (), s32[]{:S(2)}) async-start(), calls=%async_computation.4 | async-start | bytes 1966080 | tf_op jit(solution)/shard_map/reduce_scatter | solution.py:72
Sparse Core Ops, SparseCore 0:
  12.8 34.1 reduce-scatter.2
  49.1 16.8 all-gather.1
  82.6 25.7 reduce-scatter.4
where the time goes:
time: 117 us
  blocking collectives  46.1 us (39%)
  waiting for transfers between devices  35.9 us (31%)
  between operations  14.5 us (12%)
  matrix products  13.6 us (12%)
  other arithmetic  3.54 us (3%)
  local copies, waits for them, and re-layouts  2.83 us (2%)
    psum x1, blocking collectives, body(): lax.psum(lax.cond(touches(offsets, breadth, 0, span_rows * lax.axis_size(...  30.5 us
    reduce_scatter x1, waiting for transfers between devices, body(): lax.psum_scatter(feature_parts, 'tensor', scatter_dimension=1, tiled=True)  22.4 us
    all_gather x1, blocking collectives, body(): shard_rows = lax.all_gather(reduced, 'seq', axis=0, tiled=True)  15.6 us
    reduce_scatter x1, waiting for transfers between devices, body(): lax.psum_scatter(lax.dot_general(w_up, d_up, (((1,), (1,)), ((), ())), pr...  13.4 us
    dot_general x1, matrix products, body(): lax.dot_general(w_up, d_up, (((1,), (1,)), ((), ())), preferred_element_t...  3.86 us
    dot_general x1, matrix products, body(): jnp.dot(gathered, w_up, preferred_element_type=jnp.float32)  3.45 us
    dot_general x1, matrix products, body(): lax.dot_general(d_reduced, w_in, (((1,), (1,)), ((), ())), preferred_elem...  3.22 us
    unnamed x10, local copies, waits for them, and re-layouts  2.83 us
  transfers between devices with their start and end apart: 3, of which 2 were waited for; matrix products, arithmetic and copies ran while one was open for 10% of the time, Pallas kernels for 0%

commit v1 on v0

--- a/solution.py
+++ b/solution.py
@@ -58,12 +58,10 @@
     def nothing(operand):
         return jnp.zeros((span_rows * lax.axis_size("seq"), feature_count), jnp.float32)
 
-    every_row = lax.psum(
-        lax.cond(
-            touches(offsets, breadth, 0, span_rows * lax.axis_size("seq")), compute, nothing, 0
-        ),
-        "seq",
+    here_x = lax.cond(
+        touches(offsets, breadth, 0, span_rows * lax.axis_size("seq")), compute, nothing, 0
     )
+    every_row = lax.all_gather(here_x, "seq").sum(axis=0)
     d_reduced = lax.dynamic_slice_in_dim(every_row, lax.axis_index("seq") * span_rows, span_rows, 0)
     d_reduced = d_reduced.astype(jnp.bfloat16)
     feature_parts = lax.dot_general(

time: 117 us -> 154 us (1.32)
  waiting for transfers between devices: 35.9 us -> 101 us
  blocking collectives: 46.1 us -> 15.2 us
  other arithmetic: 3.54 us -> 5.29 us
    psum x1 -> x0, blocking collectives: 30.5 us -> none  [body(): lax.psum(lax.cond(touches(offsets, breadth, 0, span_rows * lax.axis_size(...]
    all_gather x0 -> x1, waiting for transfers between devices: none -> 29.5 us  [body(): every_row = lax.all_gather(here_x, 'seq').sum(axis=0)]
    reduce_scatter x1, waiting for transfers between devices: 13.4 us -> 32.4 us  [body(): lax.psum_scatter(lax.dot_general(w_up, d_up, (((1,), (1,)), ((), ())), pr...]
    all_gather x1, waiting for transfers between devices: 0.02 us -> 12.1 us  [body(): gathered = lax.all_gather(upsampled, 'tensor', axis=1, tiled=True)]
    reduce_scatter x1, waiting for transfers between devices: 22.4 us -> 27.3 us  [body(): lax.psum_scatter(feature_parts, 'tensor', scatter_dimension=1, tiled=True)]
    reduce_sum x0 -> x1, other arithmetic: none -> 1.74 us  [body(): every_row = lax.all_gather(here_x, 'seq').sum(axis=0)]
    unnamed x10 -> x12, local copies, waits for them, and re-layouts: 2.83 us -> 3.6 us
  transfers between devices with their start and end apart: 3 -> 4, of which waited for: 2 -> 4; matrix products, arithmetic and copies ran while one was open for 10% -> 7% of each run, Pallas kernels for 0% -> 0%
where the time goes in v1:
time: 154 us
  waiting for transfers between devices  101 us (66%)
  blocking collectives  15.2 us (10%)
  between operations  14.5 us (9%)
  matrix products  13.6 us (9%)
  other arithmetic  5.29 us (3%)
  local copies, waits for them, and re-layouts  3.6 us (2%)
    reduce_scatter x1, waiting for transfers between devices, body(): lax.psum_scatter(lax.dot_general(w_up, d_up, (((1,), (1,)), ((), ())), pr...  32.4 us
    all_gather x1, waiting for transfers between devices, body(): every_row = lax.all_gather(here_x, 'seq').sum(axis=0)  29.5 us
    reduce_scatter x1, waiting for transfers between devices, body(): lax.psum_scatter(feature_parts, 'tensor', scatter_dimension=1, tiled=True)  27.3 us
    all_gather x1, blocking collectives, body(): shard_rows = lax.all_gather(reduced, 'seq', axis=0, tiled=True)  15.2 us
    all_gather x1, waiting for transfers between devices, body(): gathered = lax.all_gather(upsampled, 'tensor', axis=1, tiled=True)  12.1 us
    dot_general x1, matrix products, body(): lax.dot_general(w_up, d_up, (((1,), (1,)), ((), ())), preferred_element_t...  3.84 us
    unnamed x12, local copies, waits for them, and re-layouts  3.6 us
    dot_general x1, matrix products, body(): jnp.dot(gathered, w_up, preferred_element_type=jnp.float32)  3.45 us
  transfers between devices with their start and end apart: 4, of which 4 were waited for; matrix products, arithmetic and copies ran while one was open for 7% of the time, Pallas kernels for 0%

profile of v1, /device:TPU:0, one launch (start us, length us, event | category | flops | bytes accessed | tf_op | source)
XLA Modules:
  0.0 153.7 jit_solution(10807686938678226894)
XLA Ops:
  7.2 1.5 copy-done
  8.8 3.8 %fusion.6 = f32[1024,512]{1,0:T(8,128)} fusion(bf16[1024,1024]{1,0:T(8,128)(2,1)S(1)} %copy-done, bf16[512,1024]{1,0:T(8,128)(2,1)} %param.15), kind=kOutput, calls=%fused_computation.16 | convolution fusion | flops 1073741824 | bytes 5242880 | tf_op jit(solution)/shard_map/dot_general | solution.py:46
  12.7 0.6 copy-done.5
  13.3 0.6 and_reduce_fusion
  14.5 32.4 %reduce-scatter.3.cloned.1.call-done = f32[256,512]{1,0:T(8,128)} async-done(((f32[1024,512]{1,0:T(8,128)}), f32[256,512]{1,0:T(8,128)}) %reduce-scatter.3.cloned.1.call-update) | async-done | bytes 524304 | tf_op jit(solution)/shard_map/reduce_scatter | solution.py:45
  46.9 1.1 convert_element_type.40
  48.0 0.8 conditional.3
  48.0 0.1 iota_subtract_fusion.1
  48.1 0.3 convolution_convert_fusion.1
  48.4 0.3 fusion.5
  48.8 0.8 copy-done.1
  49.7 1.8 %convolution_convert_fusion.3 = bf16[128,256]{1,0:T(8,128)(2,1)S(1)} fusion(bf16[128,3072]{1,0:T(8,128)(2,1)S(1)} %copy-done.3, bf16[3072,256]{1,0:T(8,128)(2,1)} %param.11), kind=kOutput, calls=%fused_computation.9 | convolution fusion | flops 201359360 | bytes 2424832 | tf_op jit(solution)/shard_map/dot_general | solution.py:25
  51.5 15.2 %all_gather.12 = bf16[512,256]{1,0:T(8,128)(2,1)S(1)} all-gather(bf16[128,256]{1,0:T(8,128)(2,1)S(1)} %convolution_convert_fusion.3), channel_id=1, replica_groups=mesh['group'=2,'seq'=4,'tensor'=4] {'seq'}, dimensions={0}, use_global_device_ids=true | all-gather | bytes 327680 | tf_op jit(solution)/shard_map/all_gather | solution.py:29
  66.7 0.7 conditional.2
  66.7 0.3 convolution_convert_fusion
  67.1 0.3 fusion.4
  67.4 0.7 copy-done.2
  68.2 29.5 %all-gather.6.cloned.1.call-done = f32[2048,256]{1,0:T(8,128)} async-done(((f32[512,256]{1,0:T(8,128)}), f32[2048,256]{1,0:T(8,128)}) %all-gather.6.cloned.1.call-update) | async-done | bytes 2097168 | tf_op jit(solution)/shard_map/all_gather | solution.py:64
  97.7 1.7 %reduce_sum.9 = bf16[512,256]{1,0:T(8,128)(2,1)S(1)} reduce(f32[4,512,256]{2,1,0:T(8,128)} %bitcast.22, f32[]{:T(128)} %constant.6.clone.1), dimensions={0}, to_apply=%region_6.0 | reduce | flops 393216 | bytes 2359300 | tf_op jit(solution)/shard_map/reduce_sum | solution.py:64
  99.4 3.2 %fusion.2 = f32[128,3072]{1,0:T(8,128)} fusion(bf16[3072,256]{1,0:T(8,128)(2,1)} %param.11, bf16[512,256]{1,0:T(8,128)(2,1)S(1)} %reduce_sum.9, s32[]{:T(128)S(6)} %select_n.3), kind=kOutput, calls=%fused_computation.11 | convolution fusion | flops 201326592 | bytes 3211268 | tf_op jit(solution)/shard_map/dot_general | solution.py:67
  102.7 12.1 %all-gather.4.cloned.1.call-done = bf16[512,1024]{1,0:T(8,128)(2,1)} async-done(((bf16[512,256]{1,0:T(8,128)(2,1)}), bf16[512,1024]{1,0:T(8,128)(2,1)}) %all-gather.4.cloned.1.call-update) | async-done | bytes 1048592 | tf_op jit(solution)/shard_map/all_gather | solution.py:43
  114.7 3.4 %convolution_convert_fusion.2 = bf16[512,1024]{1,0:T(8,128)(2,1)} fusion(bf16[512,1024]{1,0:T(8,128)(2,1)} %all-gather.4.cloned.1.call-done, bf16[1024,1024]{1,0:T(8,128)(2,1)S(1)} %copy-done), kind=kOutput, calls=%fused_computation.8 | convolution fusion | flops 1074266112 | bytes 4194304 | tf_op jit(solution)/shard_map/dot_general | solution.py:44
  118.2 27.3 %reduce-scatter.5.cloned.1.call-done = f32[128,768]{1,0:T(8,128)} async-done(((f32[128,3072]{1,0:T(8,128)}), f32[128,768]{1,0:T(8,128)}) %reduce-scatter.5.cloned.1.call-update) | async-done | bytes 393232 | tf_op jit(solution)/shard_map/reduce_scatter | solution.py:70
  145.5 1.7 %convert_element_type.42 = bf16[128,768]{1,0:T(8,128)(2,1)} convert(f32[128,768]{1,0:T(8,128)} %reduce-scatter.5.cloned.1.call-done) | non-fusion elementwise | flops 98304 | bytes 589824 | tf_op jit(solution)/shard_map/convert_element_type | solution.py:70
  (17 shorter events, 0.3 us)
Async XLA Ops:
  7.2 1.6 %copy-start = (bf16[1024,1024]{1,0:T(8,128)(2,1)S(1)}, bf16[1024,1024]{1,0:T(8,128)(2,1)}, u32[]{:S(2)}) copy-start(bf16[1024,1024]{1,0:T(8,128)(2,1)} %param.14) | copy-start | bytes 6291460
  7.2 39.7 %reduce-scatter.3.cloned.1.call-start = ((), (), s32[]{:S(2)}) async-start(), calls=%async_computation.3 | async-start | bytes 2621440 | tf_op jit(solution)/shard_map/reduce_scatter | solution.py:45
  12.6 0.7 copy-start.5
  12.6 35.4 %copy-start.4 = (bf16[512,128]{1,0:T(8,128)(2,1)S(1)}, bf16[512,128]{1,0:T(8,128)(2,1)}, u32[]{:S(2)}) copy-start(bf16[512,128]{1,0:T(8,128)(2,1)} %param.12) | copy-start | bytes 393220
  12.6 37.0 %copy-start.3 = (bf16[128,3072]{1,0:T(8,128)(2,1)S(1)}, bf16[128,3072]{1,0:T(8,128)(2,1)}, u32[]{:S(2)}) copy-start(bf16[128,3072]{1,0:T(8,128)(2,1)} %param.10) | copy-start | bytes 2359300
  12.6 85.0 %all-gather.6.cloned.1.call-start = ((), (), s32[]{:S(2)}) async-start(), calls=%async_computation.5 | async-start | bytes 2621440 | tf_op jit(solution)/shard_map/all_gather | solution.py:64
  48.8 0.8 copy-start.1
  49.6 65.1 %all-gather.4.cloned.1.call-start = ((), (), s32[]{:S(2)}) async-start(), calls=%async_computation.2 | async-start | bytes 1310720 | tf_op jit(solution)/shard_map/all_gather | solution.py:43
  67.4 0.7 copy-start.2
  68.1 77.4 %reduce-scatter.5.cloned.1.call-start = ((), (), s32[]{:S(2)}) async-start(), calls=%async_computation.4 | async-start | bytes 1966080 | tf_op jit(solution)/shard_map/reduce_scatter | solution.py:70
Sparse Core Ops, SparseCore 0:
  12.8 34.1 reduce-scatter.2
  49.7 47.9 all-gather.5
  99.3 15.3 all-gather.3
  117.3 28.1 reduce-scatter.4
